TPU v7x, 128 devices: a whole 4x4x4 slice. The times are simulated.
128 devices in a mesh: req: 16 (over x, y), head: 8 (over z, core).
Axes of the slice: x: 4, y: 4, z: 4, core: 2. Of those that a mesh axis runs over, the one named last changes fastest.
Arguments:
- streams: bfloat16 [12288, 4, 2048], P('req', None, 'head'), may hold values from -6 to 6
- hc_in: float32 [2, 4], replicated, may hold values from 0.2 to 1
- hc_mix: float32 [2, 4, 4], replicated, may hold values from -0.4 to 0.4
- hc_out: float32 [2, 4], replicated, may hold values from 0.5 to 1.5
- qkv_weight: bfloat16 [2048, 3, 2048], P(None, None, 'head'), may hold values from -0.125 to 0.125
- out_weight: bfloat16 [2048, 2048], P('head'), may hold values from -0.125 to 0.125
- up_gate: bfloat16 [2048, 2, 8192], P(None, None, 'head'), may hold values from -0.125 to 0.125
- down_weight: bfloat16 [8192, 2048], P('head'), may hold values from -0.0625 to 0.0625
- draft_weight: bfloat16 [2, 2048, 2048], P(None, None, 'head'), may hold values from -0.125 to 0.125
- lm_head: bfloat16 [2048, 50304], P(None, ('req', 'head')), may hold values from -0.125 to 0.125
- k_pages: bfloat16 [768, 128, 16, 128], P('req', None, 'head'), may hold values from -45 to 45
- v_pages: bfloat16 [768, 128, 16, 128], P('req', None, 'head'), may hold values from -6 to 6
- page_owner: int32 [768], P('req'), may hold values from -1 to 255, as said below
- page_fill: int32 [768], P('req'), may hold values from 0 to 128, as said below
- cache_len: int32 [256], P('req'), may hold values from 1 to 16384, as said below
- tree_parent: int32 [256, 48], P('req'), may hold values from 0 to 46, as said below
- accepted_index: int32 [256], P('req'), may hold values from 0 to 47
Outputs:
- new_streams: bfloat16 [12288, 4, 2048], P('req', None, 'head')
- logits: float32 [256, 2, 50304], P(('req', 'head'))
Inputs may be any that keep to these rules, and one draw needn't show every extreme that they name: `page_owner`: each page slot holds one page of the request it names, or -1 where it is empty. Every request owns at least one page and one request owns 128 pages; the live pages of a device's slots vary widely from device to device. `page_fill`: 0 for an empty slot; every page of a request is full except at most one. `cache_len`: equals the valid entries of the pages the request owns; one request has exactly 16384. `tree_parent`: entry i names a smaller position, the parent of position i; position 0 is the root and names itself.
All inputs are finite; a program needn't handle non-finite values.
Results may differ from a plain program's by a relative error of at most 0.027.
Values may be sent and summed in bfloat16 or wider, within the bound.
A program may use at most 512 MiB of HBM per device.

v0:
```python
import math
import jax
import jax.numpy as jnp
from jax import lax
from jax.sharding import PartitionSpec as P

NEG_FILL = -1e30
PRECISE = lax.Precision.HIGHEST


def layer_norm(values):
    center = jnp.mean(values, axis=-1, keepdims=True)
    square = jnp.mean(values * values, axis=-1, keepdims=True)
    return (values - center) * lax.rsqrt(square - center * center + 1e-05)


def normalize(values, sums, squares, width):
    center = sums / width
    return (values - center) * lax.rsqrt(squares / width - center * center + 1e-05)


def ancestors(parents):
    length = parents.shape[1]
    places = jnp.arange(length, dtype=jnp.int32)
    linked = (parents[:, :, None] == places[None, None, :]) | (places[:, None] == places[None, :])[
        None
    ]
    reach = linked.astype(jnp.float32)
    for repeat in range(max(1, (length - 1).bit_length())):
        reach = jnp.minimum(jnp.einsum("jik,jkl->jil", reach, reach, precision=PRECISE), 1.0)
    return reach


def rotate(values, positions):
    half = values.shape[-1] // 2
    freqs = jnp.exp(
        jnp.arange(half, dtype=jnp.float32) * (-2.0 * math.log(10000.0) / values.shape[-1])
    )
    angles = positions.astype(jnp.float32)[:, None] * freqs[None, :]
    cosine = jnp.cos(angles)[:, None, :]
    sine = jnp.sin(angles)[:, None, :]
    first = values[..., :half]
    second = values[..., half:]
    return jnp.concatenate(
        [first * cosine - second * sine, second * cosine + first * sine], axis=-1
    )


def blend(stream_vals, weights):
    total = weights[0] * stream_vals[:, 0]
    for index in range(1, stream_vals.shape[1]):
        total = total + weights[index] * stream_vals[:, index]
    return total


def remix(stream_vals, mixing, out_scale, delta):
    count = stream_vals.shape[1]
    matrix = jnp.eye(count, dtype=jnp.float32) + mixing
    rows = [
        blend(stream_vals, matrix[:, target]) + out_scale[target] * delta for target in range(count)
    ]
    return jnp.stack(rows, axis=1)


def stream_total(stream_vals):
    total = stream_vals[:, 0]
    for index in range(1, stream_vals.shape[1]):
        total = total + stream_vals[:, index]
    return total


def fold_rows(weight, piece):
    return jnp.dot(piece, weight, preferred_element_type=jnp.float32)


def on_device(
    streams,
    hc_in,
    hc_mix,
    hc_out,
    qkv_weight,
    out_weight,
    up_gate,
    down_weight,
    draft_weight,
    lm_head,
    k_pages,
    v_pages,
    page_owner,
    page_fill,
    cache_len,
    tree_parent,
    accepted_index,
):
    tokens_local = streams.shape[0]
    feature_local = streams.shape[2]
    width = qkv_weight.shape[0]
    req_local = cache_len.shape[0]
    tree_size = tree_parent.shape[1]
    slot_count = k_pages.shape[0]
    page_size = k_pages.shape[1]
    heads_local = k_pages.shape[2]
    head_dim = k_pages.shape[3]
    draft_count = draft_weight.shape[0]
    all_requests = req_local * lax.axis_size("req")
    reach = ancestors(tree_parent)
    depth = (jnp.sum(reach, axis=2) - 1.0).astype(jnp.int32)
    positions = (cache_len[:, None] + depth).reshape(tokens_local)
    stream_vals = streams.astype(jnp.float32)
    mixed_in = blend(stream_vals, hc_in[0])
    stat_sum, stat_square = lax.psum(
        (jnp.sum(mixed_in, axis=1), jnp.sum(mixed_in * mixed_in, axis=1)), "head"
    )
    normed = normalize(mixed_in, stat_sum[:, None], stat_square[:, None], width).astype(
        jnp.bfloat16
    )
    qkv_flat = qkv_weight.reshape(width, -1)
    projected = fold_rows(qkv_flat, lax.all_gather(normed, "head", axis=1, tiled=True))
    projected = projected.reshape(tokens_local, 3, heads_local, head_dim)
    queries = (rotate(projected[:, 0], positions) * head_dim ** (-0.5)).astype(jnp.bfloat16)
    keys_new = rotate(projected[:, 1], positions).astype(jnp.bfloat16)
    values_new = projected[:, 2].astype(jnp.bfloat16)
    gathered = lax.all_gather(
        queries.reshape(req_local, tree_size, heads_local * head_dim), "req", axis=0, tiled=True
    )
    query_all = gathered.reshape(all_requests, tree_size, heads_local, head_dim)
    safe_owner = jnp.maximum(page_owner, 0)
    live = (page_owner >= 0)[:, None] & (
        jnp.arange(page_size, dtype=jnp.int32)[None, :] < page_fill[:, None]
    )
    cache_scores = jnp.einsum(
        "pqhd,pkhd->pqhk", query_all[safe_owner], k_pages, preferred_element_type=jnp.float32
    )
    cache_scores = jnp.where(live[:, None, None, :], cache_scores, NEG_FILL)
    page_top = jnp.max(cache_scores, axis=3)
    owned_mask = page_owner[:, None] == jnp.arange(all_requests, dtype=jnp.int32)[None, :]
    owned = owned_mask.astype(jnp.float32)
    local_top = jnp.max(
        jnp.where(owned_mask[:, :, None, None], page_top[:, None], NEG_FILL), axis=0
    )
    first_request = lax.axis_index("req") * req_local
    global_top = lax.pmax(local_top.astype(jnp.bfloat16), "req").astype(local_top.dtype)
    weights = jnp.where(
        live[:, None, None, :], jnp.exp(cache_scores - global_top[safe_owner][..., None]), 0.0
    )
    page_den = jnp.sum(weights, axis=3)
    page_num = jnp.einsum(
        "pqhk,pkhd->pqhd", weights.astype(jnp.bfloat16), v_pages, preferred_element_type=jnp.float32
    )
    summed = jnp.dot(owned.T, page_num.reshape(slot_count, -1), precision=PRECISE)
    totals = jnp.dot(owned.T, page_den.reshape(slot_count, -1), precision=PRECISE)
    summed, totals = (
        summed.reshape(all_requests, tree_size, heads_local, head_dim),
        totals.reshape(all_requests, tree_size, heads_local),
    )
    own_sum, own_den = (
        lax.psum_scatter(
            summed.astype(jnp.bfloat16), "req", scatter_dimension=0, tiled=True
        ).astype(jnp.float32),
        lax.psum_scatter(
            totals.astype(jnp.bfloat16), "req", scatter_dimension=0, tiled=True
        ).astype(jnp.float32),
    )
    own_top = lax.dynamic_slice_in_dim(global_top, first_request, req_local, 0)
    query_own = queries.reshape(req_local, tree_size, heads_local, head_dim)
    keys_own = keys_new.reshape(req_local, tree_size, heads_local, head_dim)
    values_own = values_new.reshape(req_local, tree_size, heads_local, head_dim)
    tree_scores = jnp.einsum(
        "jqhd,jkhd->jqhk", query_own, keys_own, preferred_element_type=jnp.float32
    )
    tree_mask = (reach > 0)[:, :, None, :]
    tree_scores = jnp.where(tree_mask, tree_scores, NEG_FILL)
    top = jnp.maximum(own_top, jnp.max(tree_scores, axis=3))
    carried = jnp.exp(own_top - top)
    tree_weights = jnp.where(tree_mask, jnp.exp(tree_scores - top[..., None]), 0.0)
    denominator = own_den * carried + jnp.sum(tree_weights, axis=3)
    numerator = own_sum * carried[..., None] + jnp.einsum(
        "jqhk,jkhd->jqhd",
        tree_weights.astype(jnp.bfloat16),
        values_own,
        preferred_element_type=jnp.float32,
    )
    attended = (
        (numerator / denominator[..., None])
        .astype(jnp.bfloat16)
        .reshape(tokens_local, heads_local * head_dim)
    )
    attn_delta = lax.psum_scatter(
        jnp.dot(attended, out_weight, preferred_element_type=jnp.float32).astype(jnp.bfloat16),
        "head",
        scatter_dimension=1,
        tiled=True,
    ).astype(jnp.float32)
    first_streams = remix(stream_vals, hc_mix[0], hc_out[0], attn_delta)
    mixed_mid = blend(first_streams, hc_in[1])
    mid_sum, mid_square = lax.psum(
        (jnp.sum(mixed_mid, axis=1), jnp.sum(mixed_mid * mixed_mid, axis=1)), "head"
    )
    normed_mid = normalize(mixed_mid, mid_sum[:, None], mid_square[:, None], width).astype(
        jnp.bfloat16
    )
    gate_up_flat = up_gate.reshape(width, -1)
    hidden_local = gate_up_flat.shape[1] // 2
    gate_up = fold_rows(gate_up_flat, lax.all_gather(normed_mid, "head", axis=1, tiled=True))
    hidden = (jax.nn.silu(gate_up[:, :hidden_local]) * gate_up[:, hidden_local:]).astype(
        jnp.bfloat16
    )
    mlp_delta = lax.psum_scatter(
        jnp.dot(hidden, down_weight, preferred_element_type=jnp.float32).astype(jnp.bfloat16),
        "head",
        scatter_dimension=1,
        tiled=True,
    ).astype(jnp.float32)
    second_streams = remix(first_streams, hc_mix[1], hc_out[1], mlp_delta)
    new_streams = second_streams.astype(jnp.bfloat16)
    rows_taken = jnp.arange(req_local, dtype=jnp.int32) * tree_size + accepted_index
    final_local = stream_total(second_streams[rows_taken])
    final_full = lax.all_gather(final_local, "head", axis=1, tiled=True)
    final_norm = layer_norm(final_full)
    own_columns = lax.dynamic_slice_in_dim(
        final_norm, lax.axis_index("head") * feature_local, feature_local, 1
    )
    branch = jnp.einsum(
        "jd,kde->jke",
        final_norm.astype(jnp.bfloat16),
        draft_weight,
        preferred_element_type=jnp.float32,
    )
    drafted = (own_columns[:, None, :] + jax.nn.silu(branch)).astype(jnp.bfloat16)
    draft_full = lax.all_gather(drafted, "head", axis=2, tiled=True)
    draft_all = lax.all_gather(draft_full, "req", axis=0, tiled=True)
    logits_local = jnp.dot(
        draft_all.reshape(-1, width), lm_head, preferred_element_type=jnp.float32
    )
    logits_local = logits_local.reshape(all_requests, draft_count, -1)
    logits = lax.all_to_all(
        logits_local.astype(jnp.bfloat16), ("req", "head"), split_axis=0, concat_axis=2, tiled=True
    ).astype(logits_local.dtype)
    return (new_streams, logits)


def solution(mesh):
    in_specs = (
        P("req", None, "head"),
        P(),
        P(),
        P(),
        P(None, None, "head"),
        P("head", None),
        P(None, None, "head"),
        P("head", None),
        P(None, None, "head"),
        P(None, ("req", "head")),
        P("req", None, "head", None),
        P("req", None, "head", None),
        P("req"),
        P("req"),
        P("req"),
        P("req", None),
        P("req"),
    )
    out_specs = (P("req", None, "head"), P(("req", "head"), None, None))
    return jax.shard_map(
        on_device, mesh=mesh, in_specs=in_specs, out_specs=out_specs, check_vma=False
    )
```

profile of v0, /device:TPU:1, one launch (start us, length us, event | category | flops | bytes accessed | tf_op | source)
XLA Modules:
  0.0 640.3 jit_solution(18100017385552382236)
XLA Ops:
  8.9 1.7 copy_convert_fusion
  12.2 2.8 fusion.92
  16.1 14.7 %all-reduce.2 = (f32[768]{0:T(1024)S(1)}, f32[768]{0:T(1024)S(1)}) all-reduce(f32[768]{0:T(1024)S(1)} %fusion.47, f32[768]{0:T(1024)S(1)} %get-tuple-element.29), channel_id=1, replica_groups=mesh['req'=16,'head'=8] {'head'}, use_global_device_ids=true, to_apply=%region_3.0 | all-reduce | flops 1536 | bytes 12288 | tf_op jit(solution)/shard_map/psum | solution.py:111
  30.8 2.2 fusion.46
  33.0 4.7 copy.195
  43.3 23.3 %all-gather.6.cloned.1.call-done = bf16[768,2048]{1,0:T(8,128)(2,1)} async-done(((bf16[768,256]{1,0:T(8,128)(2,1)}), bf16[768,2048]{1,0:T(8,128)(2,1)}) %all-gather.6.cloned.1.call-update) | async-done | bytes 3145744 | tf_op jit(solution)/shard_map/all_gather | solution.py:118
  66.6 5.5 fusion.1
  76.1 2.0 copy.198
  78.0 2.0 convert_element_type.127
  81.5 60.3 %all-gather.8.cloned.1.call-done = bf16[256,48,256]{2,1,0:T(8,128)(2,1)} async-done(((bf16[16,48,256]{2,1,0:T(8,128)(2,1)}), bf16[256,48,256]{2,1,0:T(8,128)(2,1)}) %all-gather.8.cloned.1.call-update) | async-done | bytes 6291472 | tf_op jit(solution)/shard_map/all_gather | solution.py:123
  141.8 9.1 %copy.199 = bf16[256,48,256]{0,2,1:T(8,128)(2,1)} copy(bf16[256,48,256]{2,1,0:T(8,128)(2,1)} %all-gather.8.cloned.1.call-done) | data formatting | bytes 12582912 | tf_op jit(solution)/shard_map/all_gather | solution.py:123
  150.9 9.1 %copy.200 = bf16[256,48,2,128]{3,1,2,0:T(8,128)(2,1)} copy(bf16[256,48,2,128]{0,3,2,1:T(8,128)(2,1)} %bitcast.193) | data formatting | bytes 12582912 | tf_op jit(solution)/shard_map/reshape | solution.py:126
  160.1 4.5 gather_fusion
  164.6 5.1 bitcast_reduce_fusion
  170.6 58.9 %pmax.7 = bf16[256,48,2]{0,1,2:T(8,128)(2,1)S(1)} all-reduce(bf16[256,48,2]{0,1,2:T(8,128)(2,1)S(1)} %select_reduce_fusion), channel_id=1, replica_groups=mesh['req'=16,'head'=8] {'req'}, use_global_device_ids=true, to_apply=%region_7.8 | all-reduce | flops 24576 | bytes 98304 | tf_op jit(solution)/shard_map/pmax | solution.py:142
  230.2 3.6 fusion.12
  235.0 2.9 reshape.384
  238.0 3.3 dot_general.78
  241.3 7.3 %convolution_convert_fusion = bf16[256,48,2,128]{3,0,2,1:T(8,128)(2,1)} fusion(f32[48,2,128,48]{2,1,0,3:T(2,128)S(1)} %dot_general.78, s32[48]{0:T(128)S(1)} %copy-done.30), kind=kOutput, calls=%fused_computation.4 | convolution fusion | flops 1815097344 | bytes 8650944 | tf_op jit(solution)/shard_map/dot_general | solution.py:150
  252.2 1.9 slice.463
  257.9 1.7 concatenate.21
  260.9 3.0 fusion.98
  266.3 57.3 %all-reduce = bf16[256,48,2]{1,2,0:T(2,128)(2,1)S(1)} all-reduce(bf16[256,48,2]{1,2,0:T(2,128)(2,1)S(1)} %copy.220), channel_id=4, replica_groups=mesh['req'=16,'head'=8] {'req'}, use_global_device_ids=true, to_apply=%region_11.12.clone | all-reduce | flops 24576 | bytes 98304
  325.6 1.6 fusion.50
  327.2 12.3 %reduce-scatter.4.cloned.1.call-done = bf16[16,48,2,128]{3,0,2,1:T(8,128)(2,1)} async-done(((bf16[256,48,2,128]{3,0,2,1:T(8,128)(2,1)}), bf16[16,48,2,128]{3,0,2,1:T(8,128)(2,1)}) %reduce-scatter.4.cloned.1.call-update) | async-done | bytes 393232 | tf_op jit(solution)/shard_map/reduce_scatter | solution.py:157
  341.4 2.6 convolution_convert_fusion.2
  346.1 43.6 %reduce-scatter.6.cloned.1.call-done = bf16[768,256]{1,0:T(8,128)(2,1)} async-done(((bf16[768,2048]{1,0:T(8,128)(2,1)}), bf16[768,256]{1,0:T(8,128)(2,1)}) %reduce-scatter.6.cloned.1.call-update) | async-done | bytes 393232 | tf_op jit(solution)/shard_map/reduce_scatter | solution.py:188
  389.7 18.8 %fusion.87 = (f32[768]{0:T(1024)S(1)}, f32[768]{0:T(1024)S(1)}, f32[768,256]{1,0:T(8,128)}, f32[768,256]{1,0:T(8,128)}, f32[768,256]{1,0:T(8,128)}, /*index=5*/f32[768,256]{1,0:T(8,128)}, f32[768,256]{1,0:T(8,128)}) fusion(f32[]{:T(128)} %bitcast.60, f32[]{:T(128)} %bitcast.59, f32[]{:T(128)} %bitcast.58, f32[]{:T(128)} %bitcast.57, ...), kind=kLoop, calls=%fused_computation.157 | loop fusion | flops 9239040 | bytes 7477344 | tf_op jit(solution)/shard_map/reduce_sum | solution.py:197
  408.5 15.9 %all-reduce.1 = (f32[768]{0:T(1024)S(1)}, f32[768]{0:T(1024)S(1)}) all-reduce(f32[768]{0:T(1024)S(1)} %get-tuple-element.17, f32[768]{0:T(1024)S(1)} %get-tuple-element.16), channel_id=1, replica_groups=mesh['req'=16,'head'=8] {'head'}, use_global_device_ids=true, to_apply=%region_17.18 | all-reduce | flops 1536 | bytes 12288 | tf_op jit(solution)/shard_map/psum | solution.py:196
  424.5 2.2 multiply_convert_fusion
  427.1 10.2 %copy.237 = bf16[256,8,2,1024]{3,1,2,0:T(8,128)(2,1)} copy(bf16[256,8,2,1024]{3,2,1,0:T(2,128)(2,1)} %bitcast.195) | data formatting | bytes 16777216
  437.3 20.8 %all-gather.10.cloned.1.call-done = bf16[768,2048]{1,0:T(8,128)(2,1)} async-done(((bf16[768,256]{1,0:T(8,128)(2,1)}), bf16[768,2048]{1,0:T(8,128)(2,1)}) %all-gather.10.cloned.1.call-update) | async-done | bytes 3145744 | tf_op jit(solution)/shard_map/all_gather | solution.py:204
  458.0 10.1 %fusion.99 = f32[768,2048]{1,0:T(8,128)S(1)} fusion(bf16[768,2048]{1,0:T(8,128)(2,1)} %all-gather.10.cloned.1.call-done, bf16[2048,2048]{1,0:T(8,128)(2,1)} %bitcast.196), kind=kOutput, calls=%fused_computation.165 | convolution fusion | flops 6442450944 | bytes 17825792 | tf_op jit(solution)/shard_map/dot_general | solution.py:73
  468.2 4.9 convolution_convert_fusion.1
  474.5 31.9 %reduce-scatter.8.cloned.1.call-done = bf16[768,256]{1,0:T(8,128)(2,1)} async-done(((bf16[768,2048]{1,0:T(8,128)(2,1)}), bf16[768,256]{1,0:T(8,128)(2,1)}) %reduce-scatter.8.cloned.1.call-update) | async-done | bytes 393232 | tf_op jit(solution)/shard_map/reduce_scatter | solution.py:208
  506.5 7.7 %fusion.34 = (f32[768,1,256]{2,0,1:T(8,128)S(1)}, f32[768,1,256]{2,0,1:T(8,128)S(1)}) fusion(bf16[768,256]{1,0:T(8,128)(2,1)} %reduce-scatter.8.cloned.1.call-done, f32[768,256]{1,0:T(8,128)S(1)} %copy-done.8, f32[768,256]{1,0:T(8,128)S(1)} %copy-done.7, f32[768,256]{1,0:T(8,128)S(1)} %copy-done.6, f32[768,256]{1,0:T(8,128)S(1)} %copy-done.5, f32[]{:T(128)} %bitcast.56, ...), kind=kLoop, calls=%fused_computation.57 | loop fusion | flops 3735552 | bytes 5111848 | tf_op jit(solution)/shard_map/stack | solution.py:62
  514.2 6.8 %fusion.38 = (f32[768,1,256]{2,0,1:T(8,128)S(1)}, f32[768,1,256]{2,0,1:T(8,128)S(1)}) fusion(bf16[768,256]{1,0:T(8,128)(2,1)S(1)} %copy-done.21, f32[768,256]{1,0:T(8,128)S(1)} %copy-done.8, f32[768,256]{1,0:T(8,128)S(1)} %copy-done.7, f32[768,256]{1,0:T(8,128)S(1)} %copy-done.6, f32[768,256]{1,0:T(8,128)S(1)} %copy-done.5, f32[]{:T(128)} %bitcast.72, ...), kind=kLoop, calls=%fused_computation.61 | loop fusion | flops 3735552 | bytes 5111848 | tf_op jit(solution)/shard_map/stack | solution.py:62
  522.3 3.7 copy.225
  525.9 2.5 gather_fusion.2
  528.5 12.1 %all-gather = f32[16,1,2048]{2,1,0:T(1,128)S(1)} all-gather(f32[16,1,256]{2,1,0:T(1,128)S(1)} %slice_add_fusion), channel_id=2, replica_groups=mesh['req'=16,'head'=8] {'head'}, dimensions={2}, use_global_device_ids=true | all-gather | bytes 147456 | tf_op jit(solution)/shard_map/all_gather | solution.py:218
  541.1 2.0 add_convert_fusion.1
  543.1 13.9 %all_gather.22 = bf16[16,2,2048]{2,0,1:T(8,128)(2,1)} all-gather(bf16[16,2,256]{2,0,1:T(8,128)(2,1)S(1)} %add_convert_fusion.1), channel_id=1, replica_groups=mesh['req'=16,'head'=8] {'head'}, dimensions={2}, use_global_device_ids=true | all-gather | bytes 147456 | tf_op jit(solution)/shard_map/all_gather | solution.py:230
  557.1 43.6 %all-gather.12.cloned.1.call-done = bf16[256,2,2048]{2,0,1:T(8,128)(2,1)} async-done(((bf16[16,2,2048]{2,0,1:T(8,128)(2,1)}), bf16[256,2,2048]{2,0,1:T(8,128)(2,1)}) %all-gather.12.cloned.1.call-update) | async-done | bytes 2097168 | tf_op jit(solution)/shard_map/all_gather | solution.py:231
  600.8 3.1 fusion.20
  605.0 9.0 %all-to-all-start = ((bf16[256,2,393]{2,1,0:T(2,128)(2,1)}), bf16[256,2,393]{2,1,0:T(2,128)(2,1)}, u32[]{:S(2)}, u32[]{:S(2)}) async-start(bf16[256,2,393]{2,1,0:T(2,128)(2,1)} %copy.226), calls=%async_computation.3 | async-start | bytes 1048576 | tf_op jit(solution)/shard_map/all_to_all | solution.py:236
  614.4 2.4 copy.228
  616.8 10.5 %all-to-all-done = bf16[256,2,393]{2,1,0:T(2,128)(2,1)} async-done(((bf16[256,2,393]{2,1,0:T(2,128)(2,1)}), bf16[256,2,393]{2,1,0:T(2,128)(2,1)}, u32[]{:S(2)}, u32[]{:S(2)}) %all-to-all-start) | async-done | bytes 402464 | tf_op jit(solution)/shard_map/all_to_all | solution.py:236
  630.1 3.2 reshape.388
  (159 shorter events, 42.3 us)
Async XLA Ops:
  7.2 157.5 %copy-start = (bf16[48,128,2,128]{3,2,1,0:T(2,128)(2,1)S(1)}, bf16[48,128,2,128]{3,2,1,0:T(2,128)(2,1)}, u32[]{:S(2)}) copy-start(bf16[48,128,2,128]{3,2,1,0:T(2,128)(2,1)} %param.27) | copy-start | bytes 9437188
  7.2 59.4 %all-gather.6.cloned.1.call-start = ((), (), s32[]{:S(2)}) async-start(), calls=%async_computation.4 | async-start | bytes 3538944 | tf_op jit(solution)/shard_map/all_gather | solution.py:118
  10.5 1.6 copy-start.2
  15.0 0.9 copy-start.17
  33.0 4.8 copy-start.34
  33.0 108.8 %all-gather.8.cloned.1.call-start = ((), (), s32[]{:S(2)}) async-start(), calls=%async_computation.5 | async-start | bytes 6684672 | tf_op jit(solution)/shard_map/all_gather | solution.py:123
  37.8 3.8 copy-start.32
  72.1 2.4 copy-start.20
  72.1 1.1 copy-start.25
  72.1 1.5 copy-start.26
  73.6 6.5 %copy-start.30 = (s32[48]{0:T(128)S(1)}, s32[48]{0:T(128)}, u32[]{:S(2)}) copy-start(s32[48]{0:T(128)} %param.29) | copy-start | bytes 580
  74.5 0.7 copy-start.18
  80.0 259.5 %reduce-scatter.4.cloned.1.call-start = ((), (), s32[]{:S(2)}) async-start(), calls=%async_computation.6 | async-start | bytes 6684672 | tf_op jit(solution)/shard_map/reduce_scatter | solution.py:157
  164.6 5.1 copy-start.28
  248.6 1.0 copy-start.23
  248.6 1.3 copy-start.36
  248.6 2.5 copy-start.19
  248.6 141.2 %reduce-scatter.6.cloned.1.call-start = ((), (), s32[]{:S(2)}) async-start(), calls=%async_computation.7 | async-start | bytes 3538944 | tf_op jit(solution)/shard_map/reduce_scatter | solution.py:188
  251.6 5.2 copy-start.27
  257.9 6.3 copy-start.4
  260.9 3.1 copy-start.22
  323.6 17.8 %copy-start.24 = (bf16[256,2048]{1,0:T(8,128)(2,1)S(1)}, bf16[256,2048]{1,0:T(8,128)(2,1)}, u32[]{:S(2)}) copy-start(bf16[256,2048]{1,0:T(8,128)(2,1)} %param.22) | copy-start | bytes 3145732
  344.1 0.7 copy-start.29
  344.1 1.4 copy-start.31
  344.1 45.7 %copy-start.3 = (f32[768,4,256]{2,0,1:T(8,128)S(1)}, f32[768,4,256]{2,0,1:T(8,128)}, u32[]{:S(2)}) copy-start(f32[768,4,256]{2,0,1:T(8,128)} %copy-done.2) | copy-start | bytes 9437188
  344.1 113.9 %all-gather.10.cloned.1.call-start = ((), (), s32[]{:S(2)}) async-start(), calls=%async_computation.8 | async-start | bytes 3538944 | tf_op jit(solution)/shard_map/all_gather | solution.py:204
  426.7 79.8 %reduce-scatter.8.cloned.1.call-start = ((), (), s32[]{:S(2)}) async-start(), calls=%async_computation.9 | async-start | bytes 3538944 | tf_op jit(solution)/shard_map/reduce_scatter | solution.py:208
  458.0 10.2 %copy-start.33 = (bf16[1024,2048]{1,0:T(8,128)(2,1)S(1)}, bf16[1024,2048]{1,0:T(8,128)(2,1)}, u32[]{:S(2)}) copy-start(bf16[1024,2048]{1,0:T(8,128)(2,1)} %param.24) | copy-start | bytes 12582916
  473.1 0.7 copy-start.35
  473.1 33.3 %copy-start.5 = (f32[768,256]{1,0:T(8,128)S(1)}, f32[768,256]{1,0:T(8,128)}, u32[]{:S(2)}) copy-start(f32[768,256]{1,0:T(8,128)} %get-tuple-element.23) | copy-start | bytes 2359300
  473.1 33.3 %copy-start.6 = (f32[768,256]{1,0:T(8,128)S(1)}, f32[768,256]{1,0:T(8,128)}, u32[]{:S(2)}) copy-start(f32[768,256]{1,0:T(8,128)} %get-tuple-element.24) | copy-start | bytes 2359300
  473.1 33.3 %copy-start.7 = (f32[768,256]{1,0:T(8,128)S(1)}, f32[768,256]{1,0:T(8,128)}, u32[]{:S(2)}) copy-start(f32[768,256]{1,0:T(8,128)} %get-tuple-element.25) | copy-start | bytes 2359300
  473.1 33.3 %copy-start.8 = (f32[768,256]{1,0:T(8,128)S(1)}, f32[768,256]{1,0:T(8,128)}, u32[]{:S(2)}) copy-start(f32[768,256]{1,0:T(8,128)} %get-tuple-element.26) | copy-start | bytes 2359300
  473.2 127.6 %all-gather.12.cloned.1.call-start = ((), (), s32[]{:S(2)}) async-start(), calls=%async_computation.10 | async-start | bytes 2228224 | tf_op jit(solution)/shard_map/all_gather | solution.py:231
  506.4 7.7 %copy-start.21 = (bf16[768,256]{1,0:T(8,128)(2,1)S(1)}, bf16[768,256]{1,0:T(8,128)(2,1)}, u32[]{:S(2)}) copy-start(bf16[768,256]{1,0:T(8,128)(2,1)} %reduce-scatter.8.cloned.1.call-done) | copy-start | bytes 1179652
  514.1 6.8 %copy-start.9 = (f32[768,1,256]{2,0,1:T(8,128)}, f32[768,1,256]{2,0,1:T(8,128)S(1)}, u32[]{:S(2)}) copy-start(f32[768,1,256]{2,0,1:T(8,128)S(1)} %get-tuple-element.31) | copy-start | bytes 2359300
  514.1 6.8 %copy-start.11 = (f32[768,1,256]{2,0,1:T(8,128)}, f32[768,1,256]{2,0,1:T(8,128)S(1)}, u32[]{:S(2)}) copy-start(f32[768,1,256]{2,0,1:T(8,128)S(1)} %get-tuple-element.32) | copy-start | bytes 2359300
  520.9 0.9 copy-start.13
  521.0 1.1 copy-start.15
  557.1 57.0 %copy-start.10 = (f32[768,1,256]{2,0,1:T(8,128)S(1)}, f32[768,1,256]{2,0,1:T(8,128)}, u32[]{:S(2)}) copy-start(f32[768,1,256]{2,0,1:T(8,128)} %copy-done.9) | copy-start | bytes 2359300
  557.1 57.0 %copy-start.12 = (f32[768,1,256]{2,0,1:T(8,128)S(1)}, f32[768,1,256]{2,0,1:T(8,128)}, u32[]{:S(2)}) copy-start(f32[768,1,256]{2,0,1:T(8,128)} %copy-done.11) | copy-start | bytes 2359300
  557.1 57.0 %copy-start.14 = (f32[768,1,256]{2,0,1:T(8,128)S(1)}, f32[768,1,256]{2,0,1:T(8,128)}, u32[]{:S(2)}) copy-start(f32[768,1,256]{2,0,1:T(8,128)} %copy-done.13) | copy-start | bytes 2359300
  557.1 57.0 %copy-start.16 = (f32[768,1,256]{2,0,1:T(8,128)S(1)}, f32[768,1,256]{2,0,1:T(8,128)}, u32[]{:S(2)}) copy-start(f32[768,1,256]{2,0,1:T(8,128)} %copy-done.15) | copy-start | bytes 2359300
  605.0 22.3 %all-to-all-start = ((bf16[256,2,393]{2,1,0:T(2,128)(2,1)}), bf16[256,2,393]{2,1,0:T(2,128)(2,1)}, u32[]{:S(2)}, u32[]{:S(2)}) async-start(bf16[256,2,393]{2,1,0:T(2,128)(2,1)} %copy.226), calls=%async_computation.3 | async-start | bytes 1048576 | tf_op jit(solution)/shard_map/all_to_all | solution.py:236
  614.4 18.8 %copy-start.1 = (bf16[48,128,2,128]{3,2,1,0:T(2,128)(2,1)S(1)}, bf16[48,128,2,128]{3,2,1,0:T(2,128)(2,1)}, u32[]{:S(2)}) copy-start(bf16[48,128,2,128]{3,2,1,0:T(2,128)(2,1)} %param.27) | copy-start | bytes 9437188
Sparse Core Ops, SparseCore 0:
  33.1 33.4 all-gather.5
  80.1 61.6 all-gather.7
  248.7 90.7 reduce-scatter.3
  344.2 45.4 reduce-scatter.5
  426.8 31.2 all-gather.9
  473.3 33.1 reduce-scatter.7
  557.2 43.5 all-gather.11
where the time goes:
time: 650 us; the launch traced here: 640 us
  waiting for transfers between devices  246 us (38%)
  blocking collectives  173 us (27%)
  local copies, waits for them, and re-layouts  87.2 us (13%)
  other arithmetic  55.1 us (8%)
  matrix products  53.1 us (8%)
  between operations  15.7 us (2%)
  starting transfers between devices  9.87 us (2%)
    all_gather x1, waiting for transfers between devices, on_device(): lax.all_gather(queries.reshape(req_local, tree_size, heads_local * head_d...  60.3 us
    pmax x1, blocking collectives, on_device(): lax.pmax(local_top.astype(jnp.bfloat16), 'req').astype(local_top.dtype)  58.9 us
    unnamed x1, blocking collectives  57.3 us
    all_gather x1, waiting for transfers between devices, on_device(): draft_all = lax.all_gather(draft_full, 'req', axis=0, tiled=True)  43.6 us
    reduce_scatter x1, waiting for transfers between devices, on_device(): lax.psum_scatter(jnp.dot(attended, out_weight, preferred_element_type=jnp...  43.6 us
    reduce_scatter x1, waiting for transfers between devices, on_device(): lax.psum_scatter(jnp.dot(hidden, down_weight, preferred_element_type=jnp....  31.9 us
    unnamed x79, local copies, waits for them, and re-layouts  25.5 us
    all_gather x1, waiting for transfers between devices, on_device(): lax.all_gather(normed, 'head', axis=1, tiled=True)  23.3 us
  transfers between devices with their start and end apart: 8, of which 8 were waited for; matrix products, arithmetic and copies ran while one was open for 7% of the time, Pallas kernels for 0%

commit v1 on v0

--- a/solution.py
+++ b/solution.py
@@ -6,6 +6,16 @@
 
 NEG_FILL = -1e30
 PRECISE = lax.Precision.HIGHEST
+
+
+def around_the_ring(array, mesh_axis, along):
+    size = lax.axis_size(mesh_axis)
+    block, pieces = (array, [array])
+    for _ in range(size - 1):
+        block = lax.ppermute(block, mesh_axis, [(i, (i + 1) % size) for i in range(size)])
+        pieces.insert(0, block)
+    row_of_blocks = jnp.concatenate(pieces, axis=along)
+    return jnp.roll(row_of_blocks, (lax.axis_index(mesh_axis) + 1) * array.shape[along], axis=along)
 
 
 def layer_norm(values):
@@ -227,7 +237,7 @@
         preferred_element_type=jnp.float32,
     )
     drafted = (own_columns[:, None, :] + jax.nn.silu(branch)).astype(jnp.bfloat16)
-    draft_full = lax.all_gather(drafted, "head", axis=2, tiled=True)
+    draft_full = around_the_ring(drafted, "head", 2)
     draft_all = lax.all_gather(draft_full, "req", axis=0, tiled=True)
     logits_local = jnp.dot(
         draft_all.reshape(-1, width), lm_head, preferred_element_type=jnp.float32

time: 650 us -> 667 us (1.026)
  waiting for transfers between devices: 246 us -> 267 us
  blocking collectives: 173 us -> 159 us
  starting transfers between devices: 9.87 us -> 18.3 us
    ppermute x0 -> x7, waiting for transfers between devices: none -> 18.7 us  [around_the_ring(): lax.ppermute(block, mesh_axis, [(i, (i + 1) % size) for i in range(size)])]
    all_gather x1 -> x0, blocking collectives: 13.9 us -> none  [on_device(): draft_full = lax.all_gather(drafted, 'head', axis=2, tiled=True)]
    ppermute x0 -> x7, starting transfers between devices: none -> 8.44 us  [around_the_ring(): lax.ppermute(block, mesh_axis, [(i, (i + 1) % size) for i in range(size)])]
    unnamed x79 -> x96, local copies, waits for them, and re-layouts: 25.5 us -> 25 us
  transfers between devices with their start and end apart: 8 -> 15, of which waited for: 8 -> 15; matrix products, arithmetic and copies ran while one was open for 7% -> 7% of each run, Pallas kernels for 0% -> 0%
where the time goes in v1:
time: 667 us; the launch traced here: 657 us
  waiting for transfers between devices  267 us (40%)
  blocking collectives  159 us (24%)
  local copies, waits for them, and re-layouts  87.5 us (13%)
  other arithmetic  56.3 us (8%)
  matrix products  53 us (8%)
  starting transfers between devices  18.3 us (3%)
  between operations  15.8 us (2%)
    all_gather x1, waiting for transfers between devices, on_device(): lax.all_gather(queries.reshape(req_local, tree_size, heads_local * head_d...  59.6 us
    pmax x1, blocking collectives, on_device(): lax.pmax(local_top.astype(jnp.bfloat16), 'req').astype(local_top.dtype)  58.9 us
    unnamed x1, blocking collectives  57.4 us
    all_gather x1, waiting for transfers between devices, on_device(): draft_all = lax.all_gather(draft_full, 'req', axis=0, tiled=True)  45.8 us
    reduce_scatter x1, waiting for transfers between devices, on_device(): lax.psum_scatter(jnp.dot(attended, out_weight, preferred_element_type=jnp...  43.6 us
    reduce_scatter x1, waiting for transfers between devices, on_device(): lax.psum_scatter(jnp.dot(hidden, down_weight, preferred_element_type=jnp....  32.5 us
    unnamed x96, local copies, waits for them, and re-layouts  25 us
    all_gather x1, waiting for transfers between devices, on_device(): lax.all_gather(normed, 'head', axis=1, tiled=True)  23.3 us
  transfers between devices with their start and end apart: 15, of which 15 were waited for; matrix products, arithmetic and copies ran while one was open for 7% of the time, Pallas kernels for 0%

profile of v1, /device:TPU:1, one launch (start us, length us, event | category | flops | bytes accessed | tf_op | source)
XLA Modules:
  0.0 657.2 jit_solution(7461773020739437105)
XLA Ops:
  12.2 2.8 fusion.92
  16.0 14.7 %all-reduce.2 = (f32[768]{0:T(1024)S(1)}, f32[768]{0:T(1024)S(1)}) all-reduce(f32[768]{0:T(1024)S(1)} %fusion.47, f32[768]{0:T(1024)S(1)} %get-tuple-element.29), channel_id=1, replica_groups=mesh['req'=16,'head'=8] {'head'}, use_global_device_ids=true, to_apply=%region_3.0 | all-reduce | flops 1536 | bytes 12288 | tf_op jit(solution)/shard_map/psum | solution.py:121
  30.7 2.2 fusion.46
  33.0 4.7 copy.195
  43.2 23.3 %all-gather.6.cloned.1.call-done = bf16[768,2048]{1,0:T(8,128)(2,1)} async-done(((bf16[768,256]{1,0:T(8,128)(2,1)}), bf16[768,2048]{1,0:T(8,128)(2,1)}) %all-gather.6.cloned.1.call-update) | async-done | bytes 3145744 | tf_op jit(solution)/shard_map/all_gather | solution.py:128
  66.6 5.5 fusion.1
  78.0 2.0 convert_element_type.127
  82.2 59.6 %all-gather.8.cloned.1.call-done = bf16[256,48,256]{2,1,0:T(8,128)(2,1)} async-done(((bf16[16,48,256]{2,1,0:T(8,128)(2,1)}), bf16[256,48,256]{2,1,0:T(8,128)(2,1)}) %all-gather.8.cloned.1.call-update) | async-done | bytes 6291472 | tf_op jit(solution)/shard_map/all_gather | solution.py:133
  141.8 9.2 %copy.199 = bf16[256,48,256]{0,2,1:T(8,128)(2,1)} copy(bf16[256,48,256]{2,1,0:T(8,128)(2,1)} %all-gather.8.cloned.1.call-done) | data formatting | bytes 12582912 | tf_op jit(solution)/shard_map/all_gather | solution.py:133
  151.0 9.2 %copy.200 = bf16[256,48,2,128]{3,1,2,0:T(8,128)(2,1)} copy(bf16[256,48,2,128]{0,3,2,1:T(8,128)(2,1)} %bitcast.193) | data formatting | bytes 12582912 | tf_op jit(solution)/shard_map/reshape | solution.py:136
  160.2 4.5 gather_fusion
  164.7 5.1 bitcast_reduce_fusion
  170.6 58.9 %pmax.7 = bf16[256,48,2]{0,1,2:T(8,128)(2,1)S(1)} all-reduce(bf16[256,48,2]{0,1,2:T(8,128)(2,1)S(1)} %select_reduce_fusion), channel_id=1, replica_groups=mesh['req'=16,'head'=8] {'req'}, use_global_device_ids=true, to_apply=%region_7.8 | all-reduce | flops 24576 | bytes 98304 | tf_op jit(solution)/shard_map/pmax | solution.py:152
  230.2 3.6 fusion.12
  235.1 2.9 reshape.384
  238.0 3.3 dot_general.78
  241.4 7.3 %convolution_convert_fusion = bf16[256,48,2,128]{3,0,2,1:T(8,128)(2,1)} fusion(f32[48,2,128,48]{2,1,0,3:T(2,128)S(1)} %dot_general.78, s32[48]{0:T(128)S(1)} %copy-done.31), kind=kOutput, calls=%fused_computation.4 | convolution fusion | flops 1815097344 | bytes 8650944 | tf_op jit(solution)/shard_map/dot_general | solution.py:160
  261.0 3.0 fusion.98
  266.4 57.4 %all-reduce = bf16[256,48,2]{1,2,0:T(2,128)(2,1)S(1)} all-reduce(bf16[256,48,2]{1,2,0:T(2,128)(2,1)S(1)} %copy.220), channel_id=4, replica_groups=mesh['req'=16,'head'=8] {'req'}, use_global_device_ids=true, to_apply=%region_11.12.clone | all-reduce | flops 24576 | bytes 98304
  327.4 12.3 %reduce-scatter.4.cloned.1.call-done = bf16[16,48,2,128]{3,0,2,1:T(8,128)(2,1)} async-done(((bf16[256,48,2,128]{3,0,2,1:T(8,128)(2,1)}), bf16[16,48,2,128]{3,0,2,1:T(8,128)(2,1)}) %reduce-scatter.4.cloned.1.call-update) | async-done | bytes 393232 | tf_op jit(solution)/shard_map/reduce_scatter | solution.py:167
  341.6 2.6 convolution_convert_fusion.2
  346.3 43.6 %reduce-scatter.6.cloned.1.call-done = bf16[768,256]{1,0:T(8,128)(2,1)} async-done(((bf16[768,2048]{1,0:T(8,128)(2,1)}), bf16[768,256]{1,0:T(8,128)(2,1)}) %reduce-scatter.6.cloned.1.call-update) | async-done | bytes 393232 | tf_op jit(solution)/shard_map/reduce_scatter | solution.py:198
  389.9 19.1 %fusion.87 = (f32[768]{0:T(1024)S(1)}, f32[768]{0:T(1024)S(1)}, f32[768,256]{1,0:T(8,128)}, f32[768,256]{1,0:T(8,128)}, f32[768,256]{1,0:T(8,128)}, /*index=5*/f32[768,256]{1,0:T(8,128)}, f32[768,256]{1,0:T(8,128)}) fusion(f32[]{:T(128)} %bitcast.60, f32[]{:T(128)} %bitcast.59, f32[]{:T(128)} %bitcast.58, f32[]{:T(128)} %bitcast.57, ...), kind=kLoop, calls=%fused_computation.174 | loop fusion | flops 9239040 | bytes 7477344 | tf_op jit(solution)/shard_map/reduce_sum | solution.py:207
  409.0 15.9 %all-reduce.1 = (f32[768]{0:T(1024)S(1)}, f32[768]{0:T(1024)S(1)}) all-reduce(f32[768]{0:T(1024)S(1)} %get-tuple-element.17, f32[768]{0:T(1024)S(1)} %get-tuple-element.16), channel_id=1, replica_groups=mesh['req'=16,'head'=8] {'head'}, use_global_device_ids=true, to_apply=%region_17.18 | all-reduce | flops 1536 | bytes 12288 | tf_op jit(solution)/shard_map/psum | solution.py:206
  424.9 2.1 multiply_convert_fusion
  427.6 10.2 %copy.237 = bf16[256,8,2,1024]{3,1,2,0:T(8,128)(2,1)} copy(bf16[256,8,2,1024]{3,2,1,0:T(2,128)(2,1)} %bitcast.195) | data formatting | bytes 16777216
  437.8 20.9 %all-gather.10.cloned.1.call-done = bf16[768,2048]{1,0:T(8,128)(2,1)} async-done(((bf16[768,256]{1,0:T(8,128)(2,1)}), bf16[768,2048]{1,0:T(8,128)(2,1)}) %all-gather.10.cloned.1.call-update) | async-done | bytes 3145744 | tf_op jit(solution)/shard_map/all_gather | solution.py:214
  458.6 10.2 %fusion.99 = f32[768,2048]{1,0:T(8,128)S(1)} fusion(bf16[768,2048]{1,0:T(8,128)(2,1)} %all-gather.10.cloned.1.call-done, bf16[2048,2048]{1,0:T(8,128)(2,1)} %bitcast.196), kind=kOutput, calls=%fused_computation.182 | convolution fusion | flops 6442450944 | bytes 17825792 | tf_op jit(solution)/shard_map/dot_general | solution.py:83
  468.8 4.9 convolution_convert_fusion.1
  474.6 32.5 %reduce-scatter.8.cloned.1.call-done = bf16[768,256]{1,0:T(8,128)(2,1)} async-done(((bf16[768,2048]{1,0:T(8,128)(2,1)}), bf16[768,256]{1,0:T(8,128)(2,1)}) %reduce-scatter.8.cloned.1.call-update) | async-done | bytes 393232 | tf_op jit(solution)/shard_map/reduce_scatter | solution.py:218
  507.0 7.8 %fusion.34 = (f32[768,1,256]{2,0,1:T(8,128)S(1)}, f32[768,1,256]{2,0,1:T(8,128)S(1)}) fusion(bf16[768,256]{1,0:T(8,128)(2,1)} %reduce-scatter.8.cloned.1.call-done, f32[768,256]{1,0:T(8,128)S(1)} %copy-done.16, f32[768,256]{1,0:T(8,128)S(1)} %copy-done.15, f32[768,256]{1,0:T(8,128)S(1)} %copy-done.14, f32[768,256]{1,0:T(8,128)S(1)} %copy-done.13, ...), kind=kLoop, calls=%fused_computation.57 | loop fusion | flops 3735552 | bytes 5111848 | tf_op jit(solution)/shard_map/stack | solution.py:72
  514.9 6.9 %fusion.38 = (f32[768,1,256]{2,0,1:T(8,128)S(1)}, f32[768,1,256]{2,0,1:T(8,128)S(1)}) fusion(bf16[768,256]{1,0:T(8,128)(2,1)S(1)} %copy-done.21, f32[768,256]{1,0:T(8,128)S(1)} %copy-done.16, f32[768,256]{1,0:T(8,128)S(1)} %copy-done.15, f32[768,256]{1,0:T(8,128)S(1)} %copy-done.14, f32[768,256]{1,0:T(8,128)S(1)} %copy-done.13, f32[]{:T(128)} %bitcast.72, ...), kind=kLoop, calls=%fused_computation.61 | loop fusion | flops 3735552 | bytes 5111848 | tf_op jit(solution)/shard_map/stack | solution.py:72
  523.1 3.7 copy.225
  526.8 2.5 gather_fusion.2
  529.3 12.1 %all-gather = f32[16,1,2048]{2,1,0:T(1,128)S(1)} all-gather(f32[16,1,256]{2,1,0:T(1,128)S(1)} %slice_add_fusion), channel_id=2, replica_groups=mesh['req'=16,'head'=8] {'head'}, dimensions={2}, use_global_device_ids=true | all-gather | bytes 147456 | tf_op jit(solution)/shard_map/all_gather | solution.py:228
  541.9 2.0 add_convert_fusion.1
  546.6 2.3 collective-permute-start.1
  549.7 2.3 collective-permute-start.2
  555.2 2.7 collective-permute-done.3
  558.4 3.9 collective-permute-done.4
  562.3 4.4 collective-permute-done.5
  566.7 4.4 collective-permute-done.6
  571.9 45.8 %all-gather.12.cloned.1.call-done = bf16[256,2,2048]{2,0,1:T(8,128)(2,1)} async-done(((bf16[16,2,2048]{2,0,1:T(8,128)(2,1)}), bf16[256,2,2048]{2,0,1:T(8,128)(2,1)}) %all-gather.12.cloned.1.call-update) | async-done | bytes 2097168 | tf_op jit(solution)/shard_map/all_gather | solution.py:241
  617.7 3.1 fusion.20
  622.0 9.0 %all-to-all-start = ((bf16[256,2,393]{2,1,0:T(2,128)(2,1)}), bf16[256,2,393]{2,1,0:T(2,128)(2,1)}, u32[]{:S(2)}, u32[]{:S(2)}) async-start(bf16[256,2,393]{2,1,0:T(2,128)(2,1)} %copy.226), calls=%async_computation.3 | async-start | bytes 1048576 | tf_op jit(solution)/shard_map/all_to_all | solution.py:246
  631.4 2.4 copy.228
  633.8 10.5 %all-to-all-done = bf16[256,2,393]{2,1,0:T(2,128)(2,1)} async-done(((bf16[256,2,393]{2,1,0:T(2,128)(2,1)}), bf16[256,2,393]{2,1,0:T(2,128)(2,1)}, u32[]{:S(2)}, u32[]{:S(2)}) %all-to-all-start) | async-done | bytes 402464 | tf_op jit(solution)/shard_map/all_to_all | solution.py:246
  647.0 3.2 reshape.388
  (190 shorter events, 59.1 us)
Async XLA Ops:
  7.2 157.5 %copy-start = (bf16[48,128,2,128]{3,2,1,0:T(2,128)(2,1)S(1)}, bf16[48,128,2,128]{3,2,1,0:T(2,128)(2,1)}, u32[]{:S(2)}) copy-start(bf16[48,128,2,128]{3,2,1,0:T(2,128)(2,1)} %param.27) | copy-start | bytes 9437188
  7.2 59.4 %all-gather.6.cloned.1.call-start = ((), (), s32[]{:S(2)}) async-start(), calls=%async_computation.4 | async-start | bytes 3538944 | tf_op jit(solution)/shard_map/all_gather | solution.py:128
  10.6 1.6 copy-start.2
  32.9 4.8 copy-start.35
  32.9 108.8 %all-gather.8.cloned.1.call-start = ((), (), s32[]{:S(2)}) async-start(), calls=%async_computation.5 | async-start | bytes 6684672 | tf_op jit(solution)/shard_map/all_gather | solution.py:133
  37.7 3.8 copy-start.33
  72.0 2.4 copy-start.20
  72.1 1.1 copy-start.25
  72.1 1.5 copy-start.26
  73.5 6.5 copy-start.30
  73.5 6.5 copy-start.36
  80.0 259.7 %reduce-scatter.4.cloned.1.call-start = ((), (), s32[]{:S(2)}) async-start(), calls=%async_computation.6 | async-start | bytes 6684672 | tf_op jit(solution)/shard_map/reduce_scatter | solution.py:167
  164.7 5.1 copy-start.28
  238.0 3.3 copy-start.31
  248.6 1.3 copy-start.37
  248.7 2.5 copy-start.19
  248.7 141.2 %reduce-scatter.6.cloned.1.call-start = ((), (), s32[]{:S(2)}) async-start(), calls=%async_computation.7 | async-start | bytes 3538944 | tf_op jit(solution)/shard_map/reduce_scatter | solution.py:198
  251.7 5.2 copy-start.27
  258.1 6.3 copy-start.4
  261.0 3.1 copy-start.22
  323.8 17.8 %copy-start.24 = (bf16[256,2048]{1,0:T(8,128)(2,1)S(1)}, bf16[256,2048]{1,0:T(8,128)(2,1)}, u32[]{:S(2)}) copy-start(bf16[256,2048]{1,0:T(8,128)(2,1)} %param.22) | copy-start | bytes 3145732
  344.2 1.3 copy-start.32
  344.2 45.7 %copy-start.3 = (f32[768,4,256]{2,0,1:T(8,128)S(1)}, f32[768,4,256]{2,0,1:T(8,128)}, u32[]{:S(2)}) copy-start(f32[768,4,256]{2,0,1:T(8,128)} %copy-done.2) | copy-start | bytes 9437188
  344.2 114.4 %all-gather.10.cloned.1.call-start = ((), (), s32[]{:S(2)}) async-start(), calls=%async_computation.8 | async-start | bytes 3538944 | tf_op jit(solution)/shard_map/all_gather | solution.py:214
  427.1 79.9 %reduce-scatter.8.cloned.1.call-start = ((), (), s32[]{:S(2)}) async-start(), calls=%async_computation.9 | async-start | bytes 3538944 | tf_op jit(solution)/shard_map/reduce_scatter | solution.py:218
  458.6 10.2 %copy-start.34 = (bf16[1024,2048]{1,0:T(8,128)(2,1)S(1)}, bf16[1024,2048]{1,0:T(8,128)(2,1)}, u32[]{:S(2)}) copy-start(bf16[1024,2048]{1,0:T(8,128)(2,1)} %param.24) | copy-start | bytes 12582916
  473.7 33.3 %copy-start.13 = (f32[768,256]{1,0:T(8,128)S(1)}, f32[768,256]{1,0:T(8,128)}, u32[]{:S(2)}) copy-start(f32[768,256]{1,0:T(8,128)} %get-tuple-element.23) | copy-start | bytes 2359300
  473.7 33.3 %copy-start.14 = (f32[768,256]{1,0:T(8,128)S(1)}, f32[768,256]{1,0:T(8,128)}, u32[]{:S(2)}) copy-start(f32[768,256]{1,0:T(8,128)} %get-tuple-element.24) | copy-start | bytes 2359300
  473.7 33.3 %copy-start.15 = (f32[768,256]{1,0:T(8,128)S(1)}, f32[768,256]{1,0:T(8,128)}, u32[]{:S(2)}) copy-start(f32[768,256]{1,0:T(8,128)} %get-tuple-element.25) | copy-start | bytes 2359300
  473.8 33.3 %copy-start.16 = (f32[768,256]{1,0:T(8,128)S(1)}, f32[768,256]{1,0:T(8,128)}, u32[]{:S(2)}) copy-start(f32[768,256]{1,0:T(8,128)} %get-tuple-element.26) | copy-start | bytes 2359300
  473.8 143.9 %all-gather.12.cloned.1.call-start = ((), (), s32[]{:S(2)}) async-start(), calls=%async_computation.10 | async-start | bytes 2228224 | tf_op jit(solution)/shard_map/all_gather | solution.py:241
  507.0 7.8 %copy-start.21 = (bf16[768,256]{1,0:T(8,128)(2,1)S(1)}, bf16[768,256]{1,0:T(8,128)(2,1)}, u32[]{:S(2)}) copy-start(bf16[768,256]{1,0:T(8,128)(2,1)} %reduce-scatter.8.cloned.1.call-done) | copy-start | bytes 1179652
  514.8 7.0 %copy-start.5 = (f32[768,1,256]{2,0,1:T(8,128)}, f32[768,1,256]{2,0,1:T(8,128)S(1)}, u32[]{:S(2)}) copy-start(f32[768,1,256]{2,0,1:T(8,128)S(1)} %get-tuple-element.31) | copy-start | bytes 2359300
  514.8 7.0 %copy-start.7 = (f32[768,1,256]{2,0,1:T(8,128)}, f32[768,1,256]{2,0,1:T(8,128)S(1)}, u32[]{:S(2)}) copy-start(f32[768,1,256]{2,0,1:T(8,128)S(1)} %get-tuple-element.32) | copy-start | bytes 2359300
  521.8 1.1 copy-start.11
  543.9 2.6 collective-permute-start
  546.6 3.2 collective-permute-start.1
  549.7 3.8 collective-permute-start.2
  553.5 4.4 collective-permute-start.3
  557.9 4.4 collective-permute-start.4
  562.3 4.4 collective-permute-start.5
  566.7 4.4 collective-permute-start.6
  571.9 59.1 %copy-start.6 = (f32[768,1,256]{2,0,1:T(8,128)S(1)}, f32[768,1,256]{2,0,1:T(8,128)}, u32[]{:S(2)}) copy-start(f32[768,1,256]{2,0,1:T(8,128)} %copy-done.5) | copy-start | bytes 2359300
  571.9 59.1 %copy-start.8 = (f32[768,1,256]{2,0,1:T(8,128)S(1)}, f32[768,1,256]{2,0,1:T(8,128)}, u32[]{:S(2)}) copy-start(f32[768,1,256]{2,0,1:T(8,128)} %copy-done.7) | copy-start | bytes 2359300
  571.9 59.1 %copy-start.10 = (f32[768,1,256]{2,0,1:T(8,128)S(1)}, f32[768,1,256]{2,0,1:T(8,128)}, u32[]{:S(2)}) copy-start(f32[768,1,256]{2,0,1:T(8,128)} %copy-done.9) | copy-start | bytes 2359300
  571.9 59.1 %copy-start.12 = (f32[768,1,256]{2,0,1:T(8,128)S(1)}, f32[768,1,256]{2,0,1:T(8,128)}, u32[]{:S(2)}) copy-start(f32[768,1,256]{2,0,1:T(8,128)} %copy-done.11) | copy-start | bytes 2359300
  622.0 22.3 %all-to-all-start = ((bf16[256,2,393]{2,1,0:T(2,128)(2,1)}), bf16[256,2,393]{2,1,0:T(2,128)(2,1)}, u32[]{:S(2)}, u32[]{:S(2)}) async-start(bf16[256,2,393]{2,1,0:T(2,128)(2,1)} %copy.226), calls=%async_computation.3 | async-start | bytes 1048576 | tf_op jit(solution)/shard_map/all_to_all | solution.py:246
  631.4 18.8 %copy-start.1 = (bf16[48,128,2,128]{3,2,1,0:T(2,128)(2,1)S(1)}, bf16[48,128,2,128]{3,2,1,0:T(2,128)(2,1)}, u32[]{:S(2)}) copy-start(bf16[48,128,2,128]{3,2,1,0:T(2,128)(2,1)} %param.27) | copy-start | bytes 9437188
  (5 other events, 4.2 us)
Sparse Core Ops, SparseCore 0:
  33.0 33.4 all-gather.5
  80.1 61.6 all-gather.7
  248.8 90.8 reduce-scatter.3
  344.4 45.4 reduce-scatter.5
  427.2 31.3 all-gather.9
  473.9 33.0 reduce-scatter.7
  572.0 45.6 all-gather.11
